TPU v7x, 256 devices: a whole 4x4x8 slice. The times are simulated.
256 devices in a mesh: leaf: 16 (over y, x), row: 16 (over z, core).
Axes of the slice: x: 4, y: 4, z: 8, core: 2. Of those that a mesh axis runs over, the one named last changes fastest.
Arguments:
- sigma_root: float32 [2048, 2048], P(None, 'row')
- linv_one: bfloat16 [16, 2048, 2048], P('leaf', None, 'row'), as said below
- panel_one: bfloat16 [16, 512, 2048], P('leaf', None, 'row'), may hold values from -1.25 to 1.25
- tiles_one: int32 [16, 4], replicated, may hold values from 0 to 15, as said below
- mask_one: int32 [16, 4, 16], P('leaf', None, 'row'), may hold values 0 or 1
- linv_two: bfloat16 [16, 2048, 2048], P('leaf', None, 'row'), as said below
- panel_two: bfloat16 [16, 512, 2048], P('leaf', None, 'row'), may hold values from -1.25 to 1.25
- tiles_two: int32 [16, 4], replicated, may hold values from 0 to 15, as said below
- mask_two: int32 [16, 4, 16], P('leaf', None, 'row'), may hold values 0 or 1
- parent: int32 [16], replicated, may hold values from 0 to 15
Outputs:
- sigma_one: float32 [16, 2048, 2048], P('leaf', None, 'row')
- cross_one: float32 [16, 512, 2048], P('leaf', None, 'row')
- sigma_two: float32 [16, 2048, 2048], P('leaf', None, 'row')
- cross_two: float32 [16, 512, 2048], P('leaf', None, 'row')
Inputs may be any that keep to these rules, and one draw needn't show every extreme that they name: `tiles_one`: each row holds 4 different tile numbers in increasing order. `tiles_two`: each row holds 4 different tile numbers in increasing order. `linv_one`: each block is lower triangular with a positive diagonal. `sigma_root`: symmetric. `linv_two`: each block is lower triangular with a positive diagonal.
All inputs are finite; a program needn't handle non-finite values. No bound on the sum of `mask_one` or of `mask_two` on one device may be relied on, other than what follows from the above.
Results may differ from a plain program's by a relative error of at most 0.00045.
Values may be sent and summed in bfloat16 or wider, within the bound.
No kernel may reach another device: no remote copies, remote signals or barrier semaphores. Data moves between devices by JAX's collectives and lax.ppermute only.
A program may use at most 64 MiB of HBM per device.

v0:
```python
import jax
import jax.numpy as jnp
from jax import lax
from jax.sharding import PartitionSpec as P

TILE = 128


def pattern_rows(tile_list):
    offsets = jnp.arange(TILE, dtype=jnp.int32)
    return (tile_list[..., None] * TILE + offsets).reshape(tile_list.shape[:-1] + (-1,))


def expand_mask(tile_mask):
    return jnp.repeat(jnp.repeat(tile_mask, TILE, axis=0), TILE, axis=1)


def assemble(selected, row_list):
    gathered = lax.all_gather(selected, "row", axis=1, tiled=True)
    return jnp.take(gathered, row_list, axis=1)


def solve_block(selected, row_list, linv_local, panel_local, mask_local):
    select = assemble(selected, row_list)
    masked = panel_local * expand_mask(mask_local).astype(jnp.bfloat16)
    linv_wide = linv_local.astype(jnp.float32)
    whole_panel = lax.all_gather(masked, "row", axis=1, tiled=True)
    upper_part = jnp.dot(whole_panel, linv_local, preferred_element_type=jnp.float32)
    cross = -jnp.dot(select, upper_part, precision=lax.Precision.HIGHEST)
    middle = linv_wide - jnp.dot(
        whole_panel.astype(jnp.float32).T, cross, precision=lax.Precision.HIGHEST
    )
    sigma = jnp.dot(
        lax.all_gather(linv_local, "row", axis=1, tiled=True).astype(jnp.float32).T,
        middle,
        precision=lax.Precision.HIGHEST,
    )
    return (sigma, cross)


def body(
    sigma_root,
    linv_one,
    panel_one,
    tiles_one,
    mask_one,
    linv_two,
    panel_two,
    tiles_two,
    mask_two,
    parent,
):
    leaf_id = lax.axis_index("leaf")
    width = sigma_root.shape[1]
    own_tiles = lax.dynamic_index_in_dim(tiles_one, leaf_id, 0, keepdims=False)
    rows_first = pattern_rows(own_tiles)
    selected_first = jnp.take(sigma_root, rows_first, axis=0)
    sigma_first, cross_first = solve_block(
        selected_first, rows_first, linv_one[0], panel_one[0], mask_one[0]
    )
    rows_every = pattern_rows(tiles_two)
    count = rows_every.shape[0]
    block_rows = rows_every.shape[1]
    owned = (parent == leaf_id).astype(jnp.float32)
    slots = jnp.take(sigma_first, rows_every.reshape(-1), axis=0).reshape(count, block_rows, width)
    slots = slots * owned[:, None, None]
    arrived = lax.all_to_all(slots, "leaf", split_axis=0, concat_axis=0, tiled=True)
    selected_second = jnp.sum(arrived, axis=0)
    rows_second = lax.dynamic_index_in_dim(rows_every, leaf_id, 0, keepdims=False)
    sigma_second, cross_second = solve_block(
        selected_second, rows_second, linv_two[0], panel_two[0], mask_two[0]
    )
    return (sigma_first[None], cross_first[None], sigma_second[None], cross_second[None])


def solution(mesh):
    return jax.shard_map(
        body,
        mesh=mesh,
        in_specs=(
            P(None, "row"),
            P("leaf", None, "row"),
            P("leaf", None, "row"),
            P(),
            P("leaf", None, "row"),
            P("leaf", None, "row"),
            P("leaf", None, "row"),
            P(),
            P("leaf", None, "row"),
            P(),
        ),
        out_specs=(
            P("leaf", None, "row"),
            P("leaf", None, "row"),
            P("leaf", None, "row"),
            P("leaf", None, "row"),
        ),
        check_vma=False,
    )
```

profile of v0, /device:TPU:1, one launch (start us, length us, event | category | flops | bytes accessed | tf_op | source)
XLA Modules:
  0.0 404.3 jit_solution(16791441184361963141)
XLA Ops:
  7.2 0.0 copy-start
  7.2 0.0 copy-start.1
  7.2 0.0 all-gather.9.cloned.1.call-start
  7.2 0.8 convert_bitcast_fusion.1
  8.0 0.1 broadcast_bitcast_fusion.1
  8.1 1.7 bitcast_multiply_fusion.1
  9.8 0.0 all-gather.9.cloned.1.call-update
  9.8 0.0 all-gather.11.cloned.1.call-start
  9.9 0.9 multiply_reduce_fusion
  10.7 0.1 iota_add_fusion.1
  10.8 0.0 copy-done
  10.8 1.0 gather_fusion
  11.9 0.1 compare_and_fusion.2
  11.9 0.8 broadcast_select_fusion
  12.8 0.0 all-gather.11.cloned.1.call-update
  12.8 0.0 all-gather.17.cloned.1.call-start
  12.9 0.7 all-gather.17.cloned.1.call-update
  13.5 0.7 broadcast_multiply_fusion
  14.2 0.1 copy.20
  14.3 0.1 compare_select_fusion.4
  14.4 0.7 compare_convert_fusion
  15.1 0.7 convert_bitcast_fusion
  15.7 0.1 broadcast_bitcast_fusion
  15.8 0.1 iota_add_fusion
  15.9 0.1 add.146
  16.1 39.5 %all-gather.9.cloned.1.call-done = bf16[512,2048]{1,0:T(8,128)(2,1)} async-done(((bf16[512,128]{1,0:T(8,128)(2,1)}), bf16[512,2048]{1,0:T(8,128)(2,1)}) %all-gather.9.cloned.1.call-update) | async-done | bytes 2097168 | tf_op jit(solution)/shard_map/all_gather | solution.py:27
  55.5 0.0 copy-done.1
  55.5 2.3 fusion.13
  57.8 48.6 %all-gather.11.cloned.1.call-done = f32[512,2048]{1,0:T(8,128)} async-done(((f32[512,128]{1,0:T(8,128)}), f32[512,2048]{1,0:T(8,128)}) %all-gather.11.cloned.1.call-update) | async-done | bytes 4194320 | tf_op jit(solution)/shard_map/all_gather | solution.py:19
  106.5 5.3 %copy.19 = f32[512,2048]{0,1:T(8,128)} copy(f32[512,2048]{1,0:T(8,128)} %all-gather.11.cloned.1.call-done) | data formatting | bytes 8388608 | tf_op jit(solution)/shard_map/all_gather | solution.py:19
  111.8 4.2 %gather_fusion.2 = f32[512,512]{1,0:T(8,128)S(1)} fusion(f32[512,2048]{0,1:T(8,128)} %copy.19, s32[1024]{0:T(1024)S(1)} %pad_clamp_fusion.1), kind=kCustom, calls=%fused_computation.clone | custom fusion | bytes 2099200 | tf_op jit(solution)/shard_map/jit(_take)/gather | solution.py:20
  116.0 1.9 convolution_negate_fusion.1
  117.9 0.0 copy-start.4
  117.9 0.7 copy-done.4
  118.6 3.9 convolution_subtract_fusion.1
  122.6 50.3 %all-gather.17.cloned.1.call-done = bf16[1,2048,2048]{2,1,0:T(8,128)(2,1)} async-done(((bf16[1,2048,128]{2,1,0:T(8,128)(2,1)}), bf16[1,2048,2048]{2,1,0:T(8,128)(2,1)}) %all-gather.17.cloned.1.call-update) | async-done | bytes 8388624 | tf_op jit(solution)/shard_map/all_gather | solution.py:34
  172.9 6.3 %fusion.2 = f32[128,2048]{1,0:T(8,128)S(1)} fusion(f32[2048,128]{1,0:T(8,128)S(1)} %convolution_subtract_fusion.1, bf16[1,2048,2048]{2,1,0:T(8,128)(2,1)} %all-gather.17.cloned.1.call-done), kind=kOutput, calls=%fused_computation.6 | convolution fusion | flops 6442450944 | bytes 10485760 | tf_op jit(solution)/shard_map/dot_general | solution.py:33
  179.1 0.3 copy.21
  179.5 27.8 %gather_fusion.1 = f32[8192,128]{1,0:T(8,128)} fusion(f32[2048,128]{1,0:T(8,128)S(1)} %copy.21, s32[8192]{0:T(1024)S(1)} %broadcast_clamp_fusion), kind=kCustom, calls=%fused_computation.3 | custom fusion | bytes 8421376 | tf_op jit(solution)/shard_map/jit(_take)/gather | solution.py:65
  207.3 5.3 %select_multiply_fusion = f32[16,512,128]{2,1,0:T(8,128)} fusion(f32[16,512,128]{2,1,0:T(8,128)} %bitcast.84, f32[16]{0:T(128)S(1)} %compare_convert_fusion, pred[16,512]{1,0:T(8,128)(4,1)S(1)} %compare_and_fusion), kind=kLoop, calls=%fused_computation.8 | loop fusion | flops 2097152 | bytes 8396864 | tf_op jit(solution)/shard_map/mul | solution.py:66
  212.5 4.7 %all-to-all-start = ((f32[16,512,128]{2,1,0:T(8,128)}), f32[16,512,128]{2,1,0:T(8,128)}, u32[]{:S(2)}, u32[]{:S(2)}) async-start(f32[16,512,128]{2,1,0:T(8,128)} %select_multiply_fusion), calls=%async_computation | async-start | bytes 8388608 | tf_op jit(solution)/shard_map/all_to_all | solution.py:67
  217.2 0.0 copy-start.2
  217.2 0.0 all-gather.13.cloned.1.call-start
  217.3 0.0 copy-done.6
  217.3 0.8 bitcast_multiply_fusion
  218.1 0.0 all-gather.13.cloned.1.call-update
  218.1 0.0 all-gather.15.cloned.1.call-start
  218.2 62.3 %all-to-all-done = f32[16,512,128]{2,1,0:T(8,128)} async-done(((f32[16,512,128]{2,1,0:T(8,128)}), f32[16,512,128]{2,1,0:T(8,128)}, u32[]{:S(2)}, u32[]{:S(2)}) %all-to-all-start) | async-done | bytes 4194336 | tf_op jit(solution)/shard_map/all_to_all | solution.py:67
  280.5 2.4 reduce_sum.9
  282.9 0.8 copy.22
  283.7 0.0 all-gather.15.cloned.1.call-update
  283.7 0.2 all-gather.19.cloned.1.call-start
  284.0 0.3 all-gather.19.cloned.1.call-update
  284.4 0.0 all-gather.13.cloned.1.call-done
  284.4 2.3 fusion.11
  286.7 1.3 copy.23
  288.0 35.5 %all-gather.15.cloned.1.call-done = f32[512,2048]{0,1:T(8,128)} async-done(((f32[512,128]{0,1:T(8,128)}), f32[512,2048]{0,1:T(8,128)}) %all-gather.15.cloned.1.call-update) | async-done | bytes 4194320 | tf_op jit(solution)/shard_map/all_gather | solution.py:19
  323.6 4.2 %gather_fusion.3 = f32[512,512]{1,0:T(8,128)S(1)} fusion(f32[512,2048]{0,1:T(8,128)} %all-gather.15.cloned.1.call-done, s32[1024]{0:T(1024)S(1)} %pad_clamp_fusion), kind=kCustom, calls=%fused_computation.1.clone | custom fusion | bytes 2099200 | tf_op jit(solution)/shard_map/jit(_take)/gather | solution.py:20
  327.8 1.9 convolution_negate_fusion
  329.7 0.0 copy-start.5
  329.7 4.0 convolution_subtract_fusion
  333.7 56.2 %all-gather.19.cloned.1.call-done = bf16[1,2048,2048]{2,1,0:T(8,128)(2,1)} async-done(((bf16[1,2048,128]{2,1,0:T(8,128)(2,1)}), bf16[1,2048,2048]{2,1,0:T(8,128)(2,1)}) %all-gather.19.cloned.1.call-update) | async-done | bytes 8388624 | tf_op jit(solution)/shard_map/all_gather | solution.py:34
  389.9 6.3 %fusion.4 = f32[1,2048,128]{1,2,0:T(8,128)S(1)} fusion(f32[2048,128]{1,0:T(8,128)S(1)} %convolution_subtract_fusion, bf16[1,2048,2048]{2,1,0:T(8,128)(2,1)} %all-gather.19.cloned.1.call-done), kind=kOutput, calls=%fused_computation.9 | convolution fusion | flops 6442450944 | bytes 10485760 | tf_op jit(solution)/shard_map/dot_general | solution.py:33
  396.2 1.3 copy.24
  (18 shorter events, 0.1 us)
Async XLA Ops:
  7.2 3.6 copy-start
  7.2 48.4 %copy-start.1 = (bf16[1,2048,128]{2,1,0:T(8,128)(2,1)S(1)}, bf16[1,2048,128]{2,1,0:T(8,128)(2,1)}, u32[]{:S(2)}) copy-start(bf16[1,2048,128]{2,1,0:T(8,128)(2,1)} %param.13) | copy-start | bytes 1572868
  7.2 48.3 %all-gather.9.cloned.1.call-start = ((), (), s32[]{:S(2)}) async-start(), calls=%async_computation.1 | async-start | bytes 2228224 | tf_op jit(solution)/shard_map/all_gather | solution.py:27
  9.8 96.7 %all-gather.11.cloned.1.call-start = ((), (), s32[]{:S(2)}) async-start(), calls=%async_computation.2 | async-start | bytes 4456448 | tf_op jit(solution)/shard_map/all_gather | solution.py:19
  12.8 160.1 %all-gather.17.cloned.1.call-start = ((), (), s32[]{:S(2)}) async-start(), calls=%async_computation.5 | async-start | bytes 8912896 | tf_op jit(solution)/shard_map/all_gather | solution.py:34
  117.9 0.7 copy-start.4
  212.5 4.8 %copy-start.6 = (bf16[1,512,128]{2,1,0:T(8,128)(2,1)S(1)}, bf16[1,512,128]{2,1,0:T(8,128)(2,1)}, u32[]{:S(2)}) copy-start(bf16[1,512,128]{2,1,0:T(8,128)(2,1)} %param.18) | copy-start | bytes 393220
  212.5 67.9 %all-to-all-start = ((f32[16,512,128]{2,1,0:T(8,128)}), f32[16,512,128]{2,1,0:T(8,128)}, u32[]{:S(2)}, u32[]{:S(2)}) async-start(f32[16,512,128]{2,1,0:T(8,128)} %select_multiply_fusion), calls=%async_computation | async-start | bytes 8388608 | tf_op jit(solution)/shard_map/all_to_all | solution.py:67
  217.2 67.2 %copy-start.2 = (bf16[1,2048,128]{2,1,0:T(8,128)(2,1)S(1)}, bf16[1,2048,128]{2,1,0:T(8,128)(2,1)}, u32[]{:S(2)}) copy-start(bf16[1,2048,128]{2,1,0:T(8,128)(2,1)} %param.17) | copy-start | bytes 1572868
  217.2 67.2 %all-gather.13.cloned.1.call-start = ((), (), s32[]{:S(2)}) async-start(), calls=%async_computation.3 | async-start | bytes 2228224 | tf_op jit(solution)/shard_map/all_gather | solution.py:27
  218.1 105.4 %all-gather.15.cloned.1.call-start = ((), (), s32[]{:S(2)}) async-start(), calls=%async_computation.4 | async-start | bytes 4456448 | tf_op jit(solution)/shard_map/all_gather | solution.py:19
  283.7 106.2 %all-gather.19.cloned.1.call-start = ((), (), s32[]{:S(2)}) async-start(), calls=%async_computation.6 | async-start | bytes 8912896 | tf_op jit(solution)/shard_map/all_gather | solution.py:34
  288.0 41.6 %copy-start.3 = (bf16[1,2048,128]{2,1,0:T(8,128)(2,1)S(1)}, bf16[1,2048,128]{2,1,0:T(8,128)(2,1)}, u32[]{:S(2)}) copy-start(bf16[1,2048,128]{2,1,0:T(8,128)(2,1)} %param.17) | copy-start | bytes 1572868
  329.7 4.0 copy-start.5
Sparse Core Ops, SparseCore 0:
  10.4 45.1 all-gather.8
  57.9 48.5 all-gather.10
  108.2 64.6 all-gather.16
  220.1 40.0 all-gather.12
  283.9 39.6 all-gather.14
  325.2 64.6 all-gather.18
where the time goes:
time: 405 us; the launch traced here: 404 us
  waiting for transfers between devices  294 us (73%)
  local copies, waits for them, and re-layouts  47.4 us (12%)
  matrix products  28.8 us (7%)
  other arithmetic  15.1 us (4%)
  between operations  14.4 us (4%)
  starting transfers between devices  5.12 us (1%)
    all_gather x2, waiting for transfers between devices, solve_block(): lax.all_gather(linv_local, 'row', axis=1, tiled=True).astype(jnp.float32)  107 us
    all_gather x2, waiting for transfers between devices, assemble(): gathered = lax.all_gather(selected, 'row', axis=1, tiled=True)  84.1 us
    all_to_all x1, waiting for transfers between devices, body(): lax.all_to_all(slots, 'leaf', split_axis=0, concat_axis=0, tiled=True)  62.3 us
    all_gather x2, waiting for transfers between devices, solve_block(): whole_panel = lax.all_gather(masked, 'row', axis=1, tiled=True)  39.5 us
    gather x1, local copies, waits for them, and re-layouts, body(): jnp.take(sigma_first, rows_every.reshape(-1), axis=0)  27.8 us
    dot_general x2, matrix products, solve_block(): jnp.dot(lax.all_gather(linv_local, 'row', axis=1, tiled=True).astype(jnp....  12.5 us
    gather x2, local copies, waits for them, and re-layouts, assemble(): return jnp.take(gathered, row_list, axis=1)  8.43 us
  transfers between devices with their start and end apart: 7, of which 6 were waited for; matrix products, arithmetic and copies ran while one was open for 10% of the time, Pallas kernels for 0%

commit v1 on v0

--- a/solution.py
+++ b/solution.py
@@ -16,7 +16,25 @@
 
 
 def assemble(selected, row_list):
-    gathered = lax.all_gather(selected, "row", axis=1, tiled=True)
+    size, place, rows = (lax.axis_size("row"), lax.axis_index("row"), selected.shape[1])
+    upward = [(i, (i + 1) % size) for i in range(size)]
+    left = [(i, (i - 1) % size) for i in range(size)]
+    gathered = jnp.zeros(
+        (*selected.shape[:1], size * rows, *selected.shape[1 + 1 :]), selected.dtype
+    )
+    gathered = lax.dynamic_update_slice_in_dim(gathered, selected, place * rows, axis=1)
+    from_left = from_right = selected
+    half = size // 2
+    for step in range(1, half + 1):
+        from_left = lax.ppermute(from_left, "row", upward)
+        gathered = lax.dynamic_update_slice_in_dim(
+            gathered, from_left, (place - step) % size * rows, axis=1
+        )
+        if step < size - half:
+            from_right = lax.ppermute(from_right, "row", left)
+            gathered = lax.dynamic_update_slice_in_dim(
+                gathered, from_right, (place + step) % size * rows, axis=1
+            )
     return jnp.take(gathered, row_list, axis=1)
 
 

time: 405 us -> 319 us (0.79)
  waiting for transfers between devices: 294 us -> 120 us
  starting transfers between devices: 5.12 us -> 68.7 us
  local copies, waits for them, and re-layouts: 47.4 us -> 71.1 us
    all_gather x2 -> x0, waiting for transfers between devices: 84.1 us -> none  [assemble(): gathered = lax.all_gather(selected, 'row', axis=1, tiled=True)]
    all_gather x2, waiting for transfers between devices: 107 us -> 39 us  [solve_block(): lax.all_gather(linv_local, 'row', axis=1, tiled=True).astype(jnp.float32)]
    ppermute x0 -> x30, starting transfers between devices: none -> 61.6 us  [the longest x14 46.8 us: assemble(): from_right = lax.ppermute(from_right, 'row', left)]
    all_gather x2, waiting for transfers between devices: 39.5 us -> 0.02 us  [solve_block(): whole_panel = lax.all_gather(masked, 'row', axis=1, tiled=True)]
    dynamic_update_slice x0 -> x32, local copies, waits for them, and re-layouts: none -> 23.2 us  [the longest x16 11.5 us: assemble(): lax.dynamic_update_slice_in_dim(gathered, from_left, (place - step) % siz...]
    ppermute x0 -> x30, waiting for transfers between devices: none -> 16.4 us  [the longest x16 14.8 us: assemble(): from_left = lax.ppermute(from_left, 'row', upward)]
    all_gather x1 -> x0, local copies, waits for them, and re-layouts: 5.34 us -> none  [assemble(): gathered = lax.all_gather(selected, 'row', axis=1, tiled=True)]
    another operation x0 -> x2, local copies, waits for them, and re-layouts: none -> 5.08 us
  transfers between devices with their start and end apart: 7 -> 35, of which waited for: 6 -> 12; matrix products, arithmetic and copies ran while one was open for 10% -> 32% of each run, Pallas kernels for 0% -> 0%
where the time goes in v1:
time: 319 us; the launch traced here: 315 us
  waiting for transfers between devices  120 us (38%)
  local copies, waits for them, and re-layouts  71.1 us (22%)
  starting transfers between devices  68.7 us (22%)
  matrix products  27.4 us (9%)
  between operations  14.6 us (5%)
  other arithmetic  13.9 us (4%)
    all_to_all x1, waiting for transfers between devices, body(): lax.all_to_all(slots, 'leaf', split_axis=0, concat_axis=0, tiled=True)  62.9 us
    ppermute x14, starting transfers between devices, assemble(): from_right = lax.ppermute(from_right, 'row', left)  46.8 us
    all_gather x2, waiting for transfers between devices, solve_block(): lax.all_gather(linv_local, 'row', axis=1, tiled=True).astype(jnp.float32)  39 us
    gather x1, local copies, waits for them, and re-layouts, body(): jnp.take(sigma_first, rows_every.reshape(-1), axis=0)  27.7 us
    ppermute x16, waiting for transfers between devices, assemble(): from_left = lax.ppermute(from_left, 'row', upward)  14.8 us
    ppermute x16, starting transfers between devices, assemble(): from_left = lax.ppermute(from_left, 'row', upward)  14.8 us
    dot_general x2, matrix products, solve_block(): jnp.dot(lax.all_gather(linv_local, 'row', axis=1, tiled=True).astype(jnp....  12.6 us
    dynamic_update_slice x16, local copies, waits for them, and re-layouts, assemble(): lax.dynamic_update_slice_in_dim(gathered, from_left, (place - step) % siz...  11.5 us
  transfers between devices with their start and end apart: 35, of which 12 were waited for; matrix products, arithmetic and copies ran while one was open for 32% of the time, Pallas kernels for 0%

profile of v1, /device:TPU:1, one launch (start us, length us, event | category | flops | bytes accessed | tf_op | source)
XLA Modules:
  0.0 315.2 jit_solution(15474487919823765811)
XLA Ops:
  7.2 0.7 convert_bitcast_fusion.1
  8.1 1.7 bitcast_multiply_fusion.1
  11.3 1.7 bitcast_multiply_fusion
  13.6 0.9 fusion.20
  14.6 1.0 gather_fusion
  15.8 3.0 collective-permute-start
  19.4 2.8 collective-permute-done
  22.2 2.5 collective-permute-start.2
  25.0 2.8 collective-permute-start.3
  27.9 1.5 collective-permute-done.2
  29.4 2.5 collective-permute-start.4
  31.9 4.8 %collective-permute-start.5 = (f32[512,128]{1,0:T(8,128)S(1)}, f32[512,128]{1,0:T(8,128)S(1)}, u32[]{:S(2)}, u32[]{:S(2)}) collective-permute-start(f32[512,128]{1,0:T(8,128)S(1)} %collective-permute-done.3), channel_id=1, source_target_pairs={{0,15},{1,0},{2,1},{3,2},{4,3},{5,4},{6,5},{7,6},{8,7},{9,8},{10,9... | collective-permute-start | bytes 786440 | tf_op jit(solution)/shard_map/ppermute | solution.py:34
  36.9 2.5 broadcast.110.clone
  39.4 0.7 constant_dynamic-update-slice_fusion.31
  40.5 4.4 %collective-permute-start.7 = (f32[512,128]{1,0:T(8,128)S(1)}, f32[512,128]{1,0:T(8,128)S(1)}, u32[]{:S(2)}, u32[]{:S(2)}) collective-permute-start(f32[512,128]{1,0:T(8,128)S(1)} %collective-permute-done.5), channel_id=1, source_target_pairs={{0,15},{1,0},{2,1},{3,2},{4,3},{5,4},{6,5},{7,6},{8,7},{9,8},{10,9... | collective-permute-start | bytes 786440 | tf_op jit(solution)/shard_map/ppermute | solution.py:34
  45.7 0.7 constant_dynamic-update-slice_fusion.29
  48.0 5.3 %collective-permute-start.9 = (f32[512,128]{1,0:T(8,128)S(1)}, f32[512,128]{1,0:T(8,128)S(1)}, u32[]{:S(2)}, u32[]{:S(2)}) collective-permute-start(f32[512,128]{1,0:T(8,128)S(1)} %collective-permute-done.7), channel_id=1, source_target_pairs={{0,15},{1,0},{2,1},{3,2},{4,3},{5,4},{6,5},{7,6},{8,7},{9,8},{10,9... | collective-permute-start | bytes 786440 | tf_op jit(solution)/shard_map/ppermute | solution.py:34
  55.0 0.7 constant_dynamic-update-slice_fusion.25
  55.9 4.4 %collective-permute-start.11 = (f32[512,128]{1,0:T(8,128)S(1)}, f32[512,128]{1,0:T(8,128)S(1)}, u32[]{:S(2)}, u32[]{:S(2)}) collective-permute-start(f32[512,128]{1,0:T(8,128)S(1)} %collective-permute-done.9), channel_id=1, source_target_pairs={{0,15},{1,0},{2,1},{3,2},{4,3},{5,4},{6,5},{7,6},{8,7},{9,8},{10,9... | collective-permute-start | bytes 786440 | tf_op jit(solution)/shard_map/ppermute | solution.py:34
  61.2 0.7 constant_dynamic-update-slice_fusion.23
  62.9 4.4 %collective-permute-start.13 = (f32[512,128]{1,0:T(8,128)S(1)}, f32[512,128]{1,0:T(8,128)S(1)}, u32[]{:S(2)}, u32[]{:S(2)}) collective-permute-start(f32[512,128]{1,0:T(8,128)S(1)} %collective-permute-done.11), channel_id=1, source_target_pairs={{0,15},{1,0},{2,1},{3,2},{4,3},{5,4},{6,5},{7,6},{8,7},{9,8},{10,9... | collective-permute-start | bytes 786440 | tf_op jit(solution)/shard_map/ppermute | solution.py:34
  67.3 0.7 constant_dynamic-update-slice_fusion.21
  69.0 0.7 constant_dynamic-update-slice_fusion.19
  70.1 0.7 constant_dynamic-update-slice_fusion.18
  70.8 0.7 constant_dynamic-update-slice_fusion.17
  71.5 3.5 %collective-permute-done.14 = f32[512,128]{1,0:T(8,128)S(1)} collective-permute-done((f32[512,128]{1,0:T(8,128)S(1)}, f32[512,128]{1,0:T(8,128)S(1)}, u32[]{:S(2)}, u32[]{:S(2)}) %collective-permute-start.14) | collective-permute-done | bytes 262176 | tf_op jit(solution)/shard_map/ppermute | solution.py:29
  75.9 4.3 %gather_fusion.2 = f32[512,512]{1,0:T(8,128)S(1)} fusion(f32[512,2048]{0,1:T(8,128)} %constant_dynamic-update-slice_fusion.16, s32[1024]{0:T(1024)S(1)} %pad_clamp_fusion.1), kind=kCustom, calls=%fused_computation.clone | custom fusion | bytes 2099200 | tf_op jit(solution)/shard_map/jit(_take)/gather | solution.py:38
  80.2 2.5 fusion.13
  82.6 1.9 convolution_negate_fusion.1
  84.6 2.3 convolution_subtract_fusion.1
  86.9 39.0 %all-gather.11.cloned.1.call-done = bf16[1,2048,2048]{2,1,0:T(8,128)(2,1)} async-done(((bf16[1,2048,128]{2,1,0:T(8,128)(2,1)}), bf16[1,2048,2048]{2,1,0:T(8,128)(2,1)}) %all-gather.11.cloned.1.call-update) | async-done | bytes 8388624 | tf_op jit(solution)/shard_map/all_gather | solution.py:52
  125.9 6.3 %fusion.2 = f32[128,2048]{1,0:T(8,128)S(1)} fusion(f32[2048,128]{1,0:T(8,128)S(1)} %convolution_subtract_fusion.1, bf16[1,2048,2048]{2,1,0:T(8,128)(2,1)} %all-gather.11.cloned.1.call-done), kind=kOutput, calls=%fused_computation.6 | convolution fusion | flops 6442450944 | bytes 10485760 | tf_op jit(solution)/shard_map/dot_general | solution.py:51
  132.5 27.7 %gather_fusion.1 = f32[8192,128]{1,0:T(8,128)} fusion(f32[2048,128]{1,0:T(8,128)S(1)} %copy.51, s32[8192]{0:T(1024)S(1)} %broadcast_clamp_fusion), kind=kCustom, calls=%fused_computation.3 | custom fusion | bytes 8421376 | tf_op jit(solution)/shard_map/jit(_take)/gather | solution.py:83
  160.2 5.3 %select_multiply_fusion = f32[16,512,128]{2,1,0:T(8,128)} fusion(f32[16,512,128]{2,1,0:T(8,128)} %bitcast.84, f32[16]{0:T(128)S(1)} %compare_convert_fusion, pred[16,512]{1,0:T(8,128)(4,1)S(1)} %compare_and_fusion), kind=kLoop, calls=%fused_computation.8 | loop fusion | flops 2097152 | bytes 8396864 | tf_op jit(solution)/shard_map/mul | solution.py:84
  165.5 6.9 %all-to-all-start = ((f32[16,512,128]{2,1,0:T(8,128)}), f32[16,512,128]{2,1,0:T(8,128)}, u32[]{:S(2)}, u32[]{:S(2)}) async-start(f32[16,512,128]{2,1,0:T(8,128)} %select_multiply_fusion), calls=%async_computation | async-start | bytes 8388608 | tf_op jit(solution)/shard_map/all_to_all | solution.py:85
  172.5 62.9 %all-to-all-done = f32[16,512,128]{2,1,0:T(8,128)} async-done(((f32[16,512,128]{2,1,0:T(8,128)}), f32[16,512,128]{2,1,0:T(8,128)}, u32[]{:S(2)}, u32[]{:S(2)}) %all-to-all-start) | async-done | bytes 4194336 | tf_op jit(solution)/shard_map/all_to_all | solution.py:85
  235.4 2.4 reduce_sum.9
  237.9 1.2 collective-permute-start.15
  239.3 3.1 collective-permute-done.15
  242.5 2.5 collective-permute-start.17
  245.2 1.1 collective-permute-start.18
  246.3 1.9 collective-permute-done.17
  248.3 2.5 collective-permute-start.19
  251.3 2.0 collective-permute-start.20
  253.3 2.3 fusion.11
  255.6 1.3 copy.55
  257.0 2.6 broadcast.110
  260.3 0.7 constant_dynamic-update-slice_fusion.14
  261.0 3.4 %collective-permute-start.22 = (f32[512,128]{0,1:T(8,128)S(1)}, f32[512,128]{0,1:T(8,128)S(1)}, u32[]{:S(2)}, u32[]{:S(2)}) collective-permute-start(f32[512,128]{0,1:T(8,128)S(1)} %collective-permute-done.20), channel_id=1, source_target_pairs={{0,15},{1,0},{2,1},{3,2},{4,3},{5,4},{6,5},{7,6},{8,7},{9,8},{10,9... | collective-permute-start | bytes 786440 | tf_op jit(solution)/shard_map/ppermute | solution.py:34
  265.1 0.7 constant_dynamic-update-slice_fusion.12
  265.9 0.7 constant_dynamic-update-slice_fusion.11
  266.9 4.3 %collective-permute-start.24 = (f32[512,128]{0,1:T(8,128)S(1)}, f32[512,128]{0,1:T(8,128)S(1)}, u32[]{:S(2)}, u32[]{:S(2)}) collective-permute-start(f32[512,128]{0,1:T(8,128)S(1)} %collective-permute-done.22), channel_id=1, source_target_pairs={{0,15},{1,0},{2,1},{3,2},{4,3},{5,4},{6,5},{7,6},{8,7},{9,8},{10,9... | collective-permute-start | bytes 786440 | tf_op jit(solution)/shard_map/ppermute | solution.py:34
  271.2 0.7 constant_dynamic-update-slice_fusion.10
  273.4 4.8 %collective-permute-start.26 = (f32[512,128]{0,1:T(8,128)S(1)}, f32[512,128]{0,1:T(8,128)S(1)}, u32[]{:S(2)}, u32[]{:S(2)}) collective-permute-start(f32[512,128]{0,1:T(8,128)S(1)} %collective-permute-done.24), channel_id=1, source_target_pairs={{0,15},{1,0},{2,1},{3,2},{4,3},{5,4},{6,5},{7,6},{8,7},{9,8},{10,9... | collective-permute-start | bytes 786440 | tf_op jit(solution)/shard_map/ppermute | solution.py:34
  278.2 0.7 constant_dynamic-update-slice_fusion.7
  279.7 0.7 constant_dynamic-update-slice_fusion.5
  280.5 4.8 %collective-permute-start.28 = (f32[512,128]{0,1:T(8,128)S(1)}, f32[512,128]{0,1:T(8,128)S(1)}, u32[]{:S(2)}, u32[]{:S(2)}) collective-permute-start(f32[512,128]{0,1:T(8,128)S(1)} %collective-permute-done.26), channel_id=1, source_target_pairs={{0,15},{1,0},{2,1},{3,2},{4,3},{5,4},{6,5},{7,6},{8,7},{9,8},{10,9... | collective-permute-start | bytes 786440 | tf_op jit(solution)/shard_map/ppermute | solution.py:34
  286.0 0.7 constant_dynamic-update-slice_fusion.3
  288.1 2.0 collective-permute-done.29
  290.8 4.2 %gather_fusion.3 = f32[512,512]{1,0:T(8,128)S(1)} fusion(f32[512,2048]{0,1:T(8,128)} %constant_dynamic-update-slice_fusion, s32[1024]{0:T(1024)S(1)} %pad_clamp_fusion), kind=kCustom, calls=%fused_computation.1.clone | custom fusion | bytes 2099200 | tf_op jit(solution)/shard_map/jit(_take)/gather | solution.py:38
  295.1 1.9 convolution_negate_fusion
  297.0 4.0 %convolution_subtract_fusion = f32[2048,128]{1,0:T(8,128)S(1)} fusion(bf16[512,2048]{1,0:T(8,128)(2,1)} %all-gather.9.cloned.1.call-done, f32[512,128]{1,0:T(8,128)S(1)} %convolution_negate_fusion, bf16[1,2048,128]{2,1,0:T(8,128)(2,1)S(1)} %copy-done.4), kind=kOutput, calls=%fused_computation.10 | convolution fusion | flops 1611137024 | bytes 3932160 | tf_op jit(solution)/shard_map/dot_general | solution.py:48
  301.0 6.3 %fusion.4 = f32[1,2048,128]{1,2,0:T(8,128)S(1)} fusion(f32[2048,128]{1,0:T(8,128)S(1)} %convolution_subtract_fusion, bf16[1,2048,2048]{2,1,0:T(8,128)(2,1)} %all-gather.13.cloned.1.call-done), kind=kOutput, calls=%fused_computation.9 | convolution fusion | flops 6442450944 | bytes 10485760 | tf_op jit(solution)/shard_map/dot_general | solution.py:51
  307.4 1.3 copy.56
  (129 shorter events, 20.3 us)
Async XLA Ops:
  7.2 7.4 %copy-start = (f32[2048,128]{1,0:T(8,128)S(1)}, f32[2048,128]{1,0:T(8,128)}, u32[]{:S(2)}) copy-start(f32[2048,128]{1,0:T(8,128)} %param.12) | copy-start | bytes 3145732
  7.2 11.9 %copy-start.9 = (s32[16,4]{0,1:T(4,128)S(1)}, s32[16,4]{0,1:T(4,128)}, u32[]{:S(2)}) copy-start(s32[16,4]{0,1:T(4,128)} %param.19) | copy-start | bytes 772
  7.2 29.5 %copy-start.10 = (s32[16]{0:T(128)S(1)}, s32[16]{0:T(128)}, u32[]{:S(2)}) copy-start(s32[16]{0:T(128)} %param.21) | copy-start | bytes 196
  7.2 73.0 %all-gather.7.cloned.1.call-start = ((), (), s32[]{:S(2)}) async-start(), calls=%async_computation.1 | async-start | bytes 2228224 | tf_op jit(solution)/shard_map/all_gather | solution.py:45
  9.8 116.1 %all-gather.11.cloned.1.call-start = ((), (), s32[]{:S(2)}) async-start(), calls=%async_computation.3 | async-start | bytes 8912896 | tf_op jit(solution)/shard_map/all_gather | solution.py:52
  10.5 242.8 %all-gather.9.cloned.1.call-start = ((), (), s32[]{:S(2)}) async-start(), calls=%async_computation.2 | async-start | bytes 2228224 | tf_op jit(solution)/shard_map/all_gather | solution.py:45
  13.0 288.0 %all-gather.13.cloned.1.call-start = ((), (), s32[]{:S(2)}) async-start(), calls=%async_computation.4 | async-start | bytes 8912896 | tf_op jit(solution)/shard_map/all_gather | solution.py:52
  15.8 6.4 %collective-permute-start = (f32[512,128]{1,0:T(8,128)S(1)}, f32[512,128]{1,0:T(8,128)S(1)}, u32[]{:S(2)}, u32[]{:S(2)}) collective-permute-start(f32[512,128]{1,0:T(8,128)S(1)} %broadcast_select_fusion), channel_id=1, source_target_pairs={{0,1},{1,2},{2,3},{3,4},{4,5},{5,6},{6,7},{7,8},{8,9},{9,10},{10,1... | collective-permute-start | bytes 786440 | tf_op jit(solution)/shard_map/ppermute | solution.py:29
  18.9 6.1 %collective-permute-start.1 = (f32[512,128]{1,0:T(8,128)S(1)}, f32[512,128]{1,0:T(8,128)S(1)}, u32[]{:S(2)}, u32[]{:S(2)}) collective-permute-start(f32[512,128]{1,0:T(8,128)S(1)} %broadcast_select_fusion), channel_id=1, source_target_pairs={{0,15},{1,0},{2,1},{3,2},{4,3},{5,4},{6,5},{7,6},{8,7},{9,8},{10,9... | collective-permute-start | bytes 786440 | tf_op jit(solution)/shard_map/ppermute | solution.py:34
  22.2 7.2 %collective-permute-start.2 = (f32[512,128]{1,0:T(8,128)S(1)}, f32[512,128]{1,0:T(8,128)S(1)}, u32[]{:S(2)}, u32[]{:S(2)}) collective-permute-start(f32[512,128]{1,0:T(8,128)S(1)} %collective-permute-done), channel_id=1, source_target_pairs={{0,1},{1,2},{2,3},{3,4},{4,5},{5,6},{6,7},{7,8},{8,9},{9,10},{10,1... | collective-permute-start | bytes 786440 | tf_op jit(solution)/shard_map/ppermute | solution.py:29
  25.0 6.9 %collective-permute-start.3 = (f32[512,128]{1,0:T(8,128)S(1)}, f32[512,128]{1,0:T(8,128)S(1)}, u32[]{:S(2)}, u32[]{:S(2)}) collective-permute-start(f32[512,128]{1,0:T(8,128)S(1)} %collective-permute-done.1), channel_id=1, source_target_pairs={{0,15},{1,0},{2,1},{3,2},{4,3},{5,4},{6,5},{7,6},{8,7},{9,8},{10,9... | collective-permute-start | bytes 786440 | tf_op jit(solution)/shard_map/ppermute | solution.py:34
  29.4 10.7 %collective-permute-start.4 = (f32[512,128]{1,0:T(8,128)S(1)}, f32[512,128]{1,0:T(8,128)S(1)}, u32[]{:S(2)}, u32[]{:S(2)}) collective-permute-start(f32[512,128]{1,0:T(8,128)S(1)} %collective-permute-done.2), channel_id=1, source_target_pairs={{0,1},{1,2},{2,3},{3,4},{4,5},{5,6},{6,7},{7,8},{8,9},{9,10},{10,1... | collective-permute-start | bytes 786440 | tf_op jit(solution)/shard_map/ppermute | solution.py:29
  31.9 8.6 %collective-permute-start.5 = (f32[512,128]{1,0:T(8,128)S(1)}, f32[512,128]{1,0:T(8,128)S(1)}, u32[]{:S(2)}, u32[]{:S(2)}) collective-permute-start(f32[512,128]{1,0:T(8,128)S(1)} %collective-permute-done.3), channel_id=1, source_target_pairs={{0,15},{1,0},{2,1},{3,2},{4,3},{5,4},{6,5},{7,6},{8,7},{9,8},{10,9... | collective-permute-start | bytes 786440 | tf_op jit(solution)/shard_map/ppermute | solution.py:34
  40.1 6.5 %collective-permute-start.6 = (f32[512,128]{1,0:T(8,128)S(1)}, f32[512,128]{1,0:T(8,128)S(1)}, u32[]{:S(2)}, u32[]{:S(2)}) collective-permute-start(f32[512,128]{1,0:T(8,128)S(1)} %collective-permute-done.4), channel_id=1, source_target_pairs={{0,1},{1,2},{2,3},{3,4},{4,5},{5,6},{6,7},{7,8},{8,9},{9,10},{10,1... | collective-permute-start | bytes 786440 | tf_op jit(solution)/shard_map/ppermute | solution.py:29
  40.5 7.5 %collective-permute-start.7 = (f32[512,128]{1,0:T(8,128)S(1)}, f32[512,128]{1,0:T(8,128)S(1)}, u32[]{:S(2)}, u32[]{:S(2)}) collective-permute-start(f32[512,128]{1,0:T(8,128)S(1)} %collective-permute-done.5), channel_id=1, source_target_pairs={{0,15},{1,0},{2,1},{3,2},{4,3},{5,4},{6,5},{7,6},{8,7},{9,8},{10,9... | collective-permute-start | bytes 786440 | tf_op jit(solution)/shard_map/ppermute | solution.py:34
  46.6 8.4 %collective-permute-start.8 = (f32[512,128]{1,0:T(8,128)S(1)}, f32[512,128]{1,0:T(8,128)S(1)}, u32[]{:S(2)}, u32[]{:S(2)}) collective-permute-start(f32[512,128]{1,0:T(8,128)S(1)} %collective-permute-done.6), channel_id=1, source_target_pairs={{0,1},{1,2},{2,3},{3,4},{4,5},{5,6},{6,7},{7,8},{8,9},{9,10},{10,1... | collective-permute-start | bytes 786440 | tf_op jit(solution)/shard_map/ppermute | solution.py:29
  48.0 7.8 %collective-permute-start.9 = (f32[512,128]{1,0:T(8,128)S(1)}, f32[512,128]{1,0:T(8,128)S(1)}, u32[]{:S(2)}, u32[]{:S(2)}) collective-permute-start(f32[512,128]{1,0:T(8,128)S(1)} %collective-permute-done.7), channel_id=1, source_target_pairs={{0,15},{1,0},{2,1},{3,2},{4,3},{5,4},{6,5},{7,6},{8,7},{9,8},{10,9... | collective-permute-start | bytes 786440 | tf_op jit(solution)/shard_map/ppermute | solution.py:34
  55.0 7.0 %collective-permute-start.10 = (f32[512,128]{1,0:T(8,128)S(1)}, f32[512,128]{1,0:T(8,128)S(1)}, u32[]{:S(2)}, u32[]{:S(2)}) collective-permute-start(f32[512,128]{1,0:T(8,128)S(1)} %collective-permute-done.8), channel_id=1, source_target_pairs={{0,1},{1,2},{2,3},{3,4},{4,5},{5,6},{6,7},{7,8},{8,9},{9,10},{10,1... | collective-permute-start | bytes 786440 | tf_op jit(solution)/shard_map/ppermute | solution.py:29
  55.9 7.0 %collective-permute-start.11 = (f32[512,128]{1,0:T(8,128)S(1)}, f32[512,128]{1,0:T(8,128)S(1)}, u32[]{:S(2)}, u32[]{:S(2)}) collective-permute-start(f32[512,128]{1,0:T(8,128)S(1)} %collective-permute-done.9), channel_id=1, source_target_pairs={{0,15},{1,0},{2,1},{3,2},{4,3},{5,4},{6,5},{7,6},{8,7},{9,8},{10,9... | collective-permute-start | bytes 786440 | tf_op jit(solution)/shard_map/ppermute | solution.py:34
  62.1 7.0 %collective-permute-start.12 = (f32[512,128]{1,0:T(8,128)S(1)}, f32[512,128]{1,0:T(8,128)S(1)}, u32[]{:S(2)}, u32[]{:S(2)}) collective-permute-start(f32[512,128]{1,0:T(8,128)S(1)} %collective-permute-done.10), channel_id=1, source_target_pairs={{0,1},{1,2},{2,3},{3,4},{4,5},{5,6},{6,7},{7,8},{8,9},{9,10},{10,1... | collective-permute-start | bytes 786440 | tf_op jit(solution)/shard_map/ppermute | solution.py:29
  62.9 7.0 %collective-permute-start.13 = (f32[512,128]{1,0:T(8,128)S(1)}, f32[512,128]{1,0:T(8,128)S(1)}, u32[]{:S(2)}, u32[]{:S(2)}) collective-permute-start(f32[512,128]{1,0:T(8,128)S(1)} %collective-permute-done.11), channel_id=1, source_target_pairs={{0,15},{1,0},{2,1},{3,2},{4,3},{5,4},{6,5},{7,6},{8,7},{9,8},{10,9... | collective-permute-start | bytes 786440 | tf_op jit(solution)/shard_map/ppermute | solution.py:34
  69.0 6.0 %collective-permute-start.14 = (f32[512,128]{1,0:T(8,128)S(1)}, f32[512,128]{1,0:T(8,128)S(1)}, u32[]{:S(2)}, u32[]{:S(2)}) collective-permute-start(f32[512,128]{1,0:T(8,128)S(1)} %collective-permute-done.12), channel_id=1, source_target_pairs={{0,1},{1,2},{2,3},{3,4},{4,5},{5,6},{6,7},{7,8},{8,9},{9,10},{10,1... | collective-permute-start | bytes 786440 | tf_op jit(solution)/shard_map/ppermute | solution.py:29
  75.9 4.3 %copy-start.3 = (bf16[1,2048,128]{2,1,0:T(8,128)(2,1)S(1)}, bf16[1,2048,128]{2,1,0:T(8,128)(2,1)}, u32[]{:S(2)}) copy-start(bf16[1,2048,128]{2,1,0:T(8,128)(2,1)} %param.13) | copy-start | bytes 1572868
  80.2 4.4 %copy-start.2 = (bf16[512,2048]{1,0:T(8,128)(2,1)S(1)}, bf16[512,2048]{1,0:T(8,128)(2,1)}, u32[]{:S(2)}) copy-start(bf16[512,2048]{1,0:T(8,128)(2,1)} %all-gather.7.cloned.1.call-done) | copy-start | bytes 6291460
  84.6 47.6 %copy-start.5 = (f32[512,128]{1,0:T(8,128)}, f32[512,128]{1,0:T(8,128)S(1)}, u32[]{:S(2)}) copy-start(f32[512,128]{1,0:T(8,128)S(1)} %convolution_negate_fusion.1) | copy-start | bytes 786436
  165.5 69.8 %all-to-all-start = ((f32[16,512,128]{2,1,0:T(8,128)}), f32[16,512,128]{2,1,0:T(8,128)}, u32[]{:S(2)}, u32[]{:S(2)}) async-start(f32[16,512,128]{2,1,0:T(8,128)} %select_multiply_fusion), calls=%async_computation | async-start | bytes 8388608 | tf_op jit(solution)/shard_map/all_to_all | solution.py:85
  172.5 80.9 %copy-start.4 = (bf16[1,2048,128]{2,1,0:T(8,128)(2,1)S(1)}, bf16[1,2048,128]{2,1,0:T(8,128)(2,1)}, u32[]{:S(2)}) copy-start(bf16[1,2048,128]{2,1,0:T(8,128)(2,1)} %param.17) | copy-start | bytes 1572868
  237.9 4.5 %collective-permute-start.15 = (f32[512,128]{0,1:T(8,128)S(1)}, f32[512,128]{0,1:T(8,128)S(1)}, u32[]{:S(2)}, u32[]{:S(2)}) collective-permute-start(f32[512,128]{0,1:T(8,128)S(1)} %copy.52), channel_id=1, source_target_pairs={{0,1},{1,2},{2,3},{3,4},{4,5},{5,6},{6,7},{7,8},{8,9},{9,10},{10,1... | collective-permute-start | bytes 786440 | tf_op jit(solution)/shard_map/ppermute | solution.py:29
  239.1 6.1 %collective-permute-start.16 = (f32[512,128]{0,1:T(8,128)S(1)}, f32[512,128]{0,1:T(8,128)S(1)}, u32[]{:S(2)}, u32[]{:S(2)}) collective-permute-start(f32[512,128]{0,1:T(8,128)S(1)} %copy.52), channel_id=1, source_target_pairs={{0,15},{1,0},{2,1},{3,2},{4,3},{5,4},{6,5},{7,6},{8,7},{9,8},{10,9... | collective-permute-start | bytes 786440 | tf_op jit(solution)/shard_map/ppermute | solution.py:34
  242.5 10.9 %copy-start.7 = (f32[512,128]{0,1:T(8,128)}, f32[512,128]{0,1:T(8,128)S(1)}, u32[]{:S(2)}) copy-start(f32[512,128]{0,1:T(8,128)S(1)} %collective-permute-done.15) | copy-start | bytes 786436
  242.5 5.8 %collective-permute-start.17 = (f32[512,128]{0,1:T(8,128)S(1)}, f32[512,128]{0,1:T(8,128)S(1)}, u32[]{:S(2)}, u32[]{:S(2)}) collective-permute-start(f32[512,128]{0,1:T(8,128)S(1)} %collective-permute-done.15), channel_id=1, source_target_pairs={{0,1},{1,2},{2,3},{3,4},{4,5},{5,6},{6,7},{7,8},{8,9},{9,10},{10,1... | collective-permute-start | bytes 786440 | tf_op jit(solution)/shard_map/ppermute | solution.py:29
  245.2 6.1 %collective-permute-start.18 = (f32[512,128]{0,1:T(8,128)S(1)}, f32[512,128]{0,1:T(8,128)S(1)}, u32[]{:S(2)}, u32[]{:S(2)}) collective-permute-start(f32[512,128]{0,1:T(8,128)S(1)} %collective-permute-done.16), channel_id=1, source_target_pairs={{0,15},{1,0},{2,1},{3,2},{4,3},{5,4},{6,5},{7,6},{8,7},{9,8},{10,9... | collective-permute-start | bytes 786440 | tf_op jit(solution)/shard_map/ppermute | solution.py:34
  248.3 8.7 %collective-permute-start.19 = (f32[512,128]{0,1:T(8,128)S(1)}, f32[512,128]{0,1:T(8,128)S(1)}, u32[]{:S(2)}, u32[]{:S(2)}) collective-permute-start(f32[512,128]{0,1:T(8,128)S(1)} %collective-permute-done.17), channel_id=1, source_target_pairs={{0,1},{1,2},{2,3},{3,4},{4,5},{5,6},{6,7},{7,8},{8,9},{9,10},{10,1... | collective-permute-start | bytes 786440 | tf_op jit(solution)/shard_map/ppermute | solution.py:29
  251.3 9.7 %collective-permute-start.20 = (f32[512,128]{0,1:T(8,128)S(1)}, f32[512,128]{0,1:T(8,128)S(1)}, u32[]{:S(2)}, u32[]{:S(2)}) collective-permute-start(f32[512,128]{0,1:T(8,128)S(1)} %collective-permute-done.18), channel_id=1, source_target_pairs={{0,15},{1,0},{2,1},{3,2},{4,3},{5,4},{6,5},{7,6},{8,7},{9,8},{10,9... | collective-permute-start | bytes 786440 | tf_op jit(solution)/shard_map/ppermute | solution.py:34
  256.9 3.3 %copy-start.8 = (f32[512,128]{0,1:T(8,128)S(1)}, f32[512,128]{0,1:T(8,128)}, u32[]{:S(2)}) copy-start(f32[512,128]{0,1:T(8,128)} %copy-done.7) | copy-start | bytes 786436
  257.0 8.2 %collective-permute-start.21 = (f32[512,128]{0,1:T(8,128)S(1)}, f32[512,128]{0,1:T(8,128)S(1)}, u32[]{:S(2)}, u32[]{:S(2)}) collective-permute-start(f32[512,128]{0,1:T(8,128)S(1)} %collective-permute-done.19), channel_id=1, source_target_pairs={{0,1},{1,2},{2,3},{3,4},{4,5},{5,6},{6,7},{7,8},{8,9},{9,10},{10,1... | collective-permute-start | bytes 786440 | tf_op jit(solution)/shard_map/ppermute | solution.py:29
  261.0 5.9 %collective-permute-start.22 = (f32[512,128]{0,1:T(8,128)S(1)}, f32[512,128]{0,1:T(8,128)S(1)}, u32[]{:S(2)}, u32[]{:S(2)}) collective-permute-start(f32[512,128]{0,1:T(8,128)S(1)} %collective-permute-done.20), channel_id=1, source_target_pairs={{0,15},{1,0},{2,1},{3,2},{4,3},{5,4},{6,5},{7,6},{8,7},{9,8},{10,9... | collective-permute-start | bytes 786440 | tf_op jit(solution)/shard_map/ppermute | solution.py:34
  265.1 6.9 %collective-permute-start.23 = (f32[512,128]{0,1:T(8,128)S(1)}, f32[512,128]{0,1:T(8,128)S(1)}, u32[]{:S(2)}, u32[]{:S(2)}) collective-permute-start(f32[512,128]{0,1:T(8,128)S(1)} %collective-permute-done.21), channel_id=1, source_target_pairs={{0,1},{1,2},{2,3},{3,4},{4,5},{5,6},{6,7},{7,8},{8,9},{9,10},{10,1... | collective-permute-start | bytes 786440 | tf_op jit(solution)/shard_map/ppermute | solution.py:29
  266.9 6.5 %collective-permute-start.24 = (f32[512,128]{0,1:T(8,128)S(1)}, f32[512,128]{0,1:T(8,128)S(1)}, u32[]{:S(2)}, u32[]{:S(2)}) collective-permute-start(f32[512,128]{0,1:T(8,128)S(1)} %collective-permute-done.22), channel_id=1, source_target_pairs={{0,15},{1,0},{2,1},{3,2},{4,3},{5,4},{6,5},{7,6},{8,7},{9,8},{10,9... | collective-permute-start | bytes 786440 | tf_op jit(solution)/shard_map/ppermute | solution.py:34
  272.0 7.0 %collective-permute-start.25 = (f32[512,128]{0,1:T(8,128)S(1)}, f32[512,128]{0,1:T(8,128)S(1)}, u32[]{:S(2)}, u32[]{:S(2)}) collective-permute-start(f32[512,128]{0,1:T(8,128)S(1)} %collective-permute-done.23), channel_id=1, source_target_pairs={{0,1},{1,2},{2,3},{3,4},{4,5},{5,6},{6,7},{7,8},{8,9},{9,10},{10,1... | collective-permute-start | bytes 786440 | tf_op jit(solution)/shard_map/ppermute | solution.py:29
  273.4 7.0 %collective-permute-start.26 = (f32[512,128]{0,1:T(8,128)S(1)}, f32[512,128]{0,1:T(8,128)S(1)}, u32[]{:S(2)}, u32[]{:S(2)}) collective-permute-start(f32[512,128]{0,1:T(8,128)S(1)} %collective-permute-done.24), channel_id=1, source_target_pairs={{0,15},{1,0},{2,1},{3,2},{4,3},{5,4},{6,5},{7,6},{8,7},{9,8},{10,9... | collective-permute-start | bytes 786440 | tf_op jit(solution)/shard_map/ppermute | solution.py:34
  279.0 7.0 %collective-permute-start.27 = (f32[512,128]{0,1:T(8,128)S(1)}, f32[512,128]{0,1:T(8,128)S(1)}, u32[]{:S(2)}, u32[]{:S(2)}) collective-permute-start(f32[512,128]{0,1:T(8,128)S(1)} %collective-permute-done.25), channel_id=1, source_target_pairs={{0,1},{1,2},{2,3},{3,4},{4,5},{5,6},{6,7},{7,8},{8,9},{9,10},{10,1... | collective-permute-start | bytes 786440 | tf_op jit(solution)/shard_map/ppermute | solution.py:29
  280.5 7.0 %collective-permute-start.28 = (f32[512,128]{0,1:T(8,128)S(1)}, f32[512,128]{0,1:T(8,128)S(1)}, u32[]{:S(2)}, u32[]{:S(2)}) collective-permute-start(f32[512,128]{0,1:T(8,128)S(1)} %collective-permute-done.26), channel_id=1, source_target_pairs={{0,15},{1,0},{2,1},{3,2},{4,3},{5,4},{6,5},{7,6},{8,7},{9,8},{10,9... | collective-permute-start | bytes 786440 | tf_op jit(solution)/shard_map/ppermute | solution.py:34
  286.0 4.2 %collective-permute-start.29 = (f32[512,128]{0,1:T(8,128)S(1)}, f32[512,128]{0,1:T(8,128)S(1)}, u32[]{:S(2)}, u32[]{:S(2)}) collective-permute-start(f32[512,128]{0,1:T(8,128)S(1)} %collective-permute-done.27), channel_id=1, source_target_pairs={{0,1},{1,2},{2,3},{3,4},{4,5},{5,6},{6,7},{7,8},{8,9},{9,10},{10,1... | collective-permute-start | bytes 786440 | tf_op jit(solution)/shard_map/ppermute | solution.py:29
  297.0 10.4 %copy-start.6 = (f32[512,128]{1,0:T(8,128)}, f32[512,128]{1,0:T(8,128)S(1)}, u32[]{:S(2)}) copy-start(f32[512,128]{1,0:T(8,128)S(1)} %convolution_negate_fusion) | copy-start | bytes 786436
  301.0 7.7 %copy-start.1 = (f32[2048,128]{1,0:T(8,128)S(1)}, f32[2048,128]{1,0:T(8,128)}, u32[]{:S(2)}) copy-start(f32[2048,128]{1,0:T(8,128)} %param.12) | copy-start | bytes 3145732
Sparse Core Ops, SparseCore 0:
  10.4 49.2 all-gather.6
  61.4 64.4 all-gather.10
  128.2 39.5 all-gather.8
  169.4 64.3 all-gather.12
